TPU v7x, 32 devices: a whole 2x2x4 slice. The times are simulated.
32 devices in a mesh: groups: 2 (over x), tm: 16 (over z, y, core).
Axes of the slice: x: 2, y: 2, z: 4, core: 2. Of those that a mesh axis runs over, the one named last changes fastest.
Arguments:
- records: bfloat16 [384, 4096], P('groups', 'tm'), parts along dimension 0, may hold values from -6 to 6
- bank: bfloat16 [256, 384, 240], P('tm', 'groups'), parts along dimension 1, may hold values from -6 to 6
- plan: int32 [6], P('groups'), parts along dimension 0, may hold values from 0 to 15
- template_ids: int32 [6, 2], P('groups'), parts along dimension 0, may hold values from 0 to 15
- channel_mask: int32 [384], P('groups'), parts along dimension 0, may hold values 0 or 1
Outputs:
- detection: float32 [6, 2, 4096], P('groups', None, 'tm'), parts along dimension 0
There are 2 independent parts, one for each index of `groups`. A program takes and returns all parts, laid end to end along the dimension named above; each array names one. Nothing has to cross between parts.
Inputs may be any that keep to these rules, and one draw needn't show every extreme that they name: `plan`: the index of tm that holds a step's templates. `template_ids`: slots within the owner's 16 templates.
All inputs are finite; a program needn't handle non-finite values.
Results may differ from a plain program's by a relative error of at most 0.0003.
Values may be sent and summed in bfloat16 or wider, within the bound.
A program may use at most 64 MiB of HBM per device.

v0:
```python
import functools

import jax
import jax.numpy as jnp
from jax import lax
from jax.experimental import pallas as pl
from jax.experimental.pallas import tpu as pltpu
from jax.sharding import PartitionSpec as P

MESH = pl.DeviceIdType.MESH
LANES = 128


def up(value, unit):
    return -(-value // unit) * unit


def kernel(
    n, steps, kcount, taps, unroll,
    plan_ref, ids_ref, mask_s, mask_v, rec_ref, bank_ref, out_ref,
    wide, rwide, tsend, tpart, tcomb, rsend, trecv, rrecv, xs, frames, inv, tmpl, wts, acc, osend, orecv, bank_v,
    bank_sem, cs_sem, cr_sem, ts_sem, tr_sem, rs_sem, rr_sem, os_sem, or_sem,
):
    me = lax.axis_index("tm")
    chip, core = me // 2, me % 2
    chips = n // 2
    partner = me + 1 - 2 * core
    chans, block = rec_ref.shape
    own = chans // n
    rows = kcount * own
    halves = block // LANES
    width = frames.shape[2] // LANES
    dims = (((1,), (1,)), ((), ()))

    barrier = pltpu.get_barrier_semaphore()

    @pl.loop(1, n)
    def _(o):
        pl.semaphore_signal(barrier, inc=1, device_id={"tm": lax.rem(me + o, n)}, device_id_type=MESH)

    fetch = pltpu.make_async_copy(bank_ref, bank_v, bank_sem)
    fetch.start()

    rec_f = rec_ref[...].astype(jnp.float32)
    for v in range(halves):
        rwide[v] = rec_f[:, v * LANES : (v + 1) * LANES]
    pad = 2 * LANES - taps
    fetch.wait()
    for s in range(steps):
        for k in range(kcount):
            pick = bank_v[ids_ref[k, s]].astype(jnp.float32)
            pick = jnp.concatenate([pick, jnp.zeros((chans, pad), jnp.float32)], axis=1)
            for v in range(2):
                wide[s, v, k * chans : (k + 1) * chans, :] = pick[:, v * LANES : (v + 1) * LANES]

    @pl.loop(0, n)
    def _(d):
        for v in range(halves):
            rsend[d, :, v * LANES : (v + 1) * LANES] = rwide[v, pl.ds(d, own, stride=n), :].astype(jnp.bfloat16)
        for s in range(steps):
            for v in range(2):
                tsend[s, d % 2, d // 2, :, v * LANES : (v + 1) * LANES] = wide[
                    s, v, pl.ds(d, rows, stride=n), :
                ].astype(jnp.bfloat16)

    rrecv[me] = rsend[me]

    def hop(send, recv, send_sem, recv_sem, o):
        to = lax.rem(me + o, n)
        return pltpu.make_async_remote_copy(
            src_ref=send.at[to], dst_ref=recv.at[me], send_sem=send_sem.at[o], recv_sem=recv_sem.at[o],
            device_id={"tm": to}, device_id_type=MESH,
        )

    def across(s):
        return pltpu.make_async_remote_copy(
            src_ref=tsend.at[s, 1 - core], dst_ref=tpart.at[s], send_sem=cs_sem.at[s], recv_sem=cr_sem.at[s],
            device_id={"tm": partner}, device_id_type=MESH,
        )

    def spread(s, o):
        to = lax.rem(chip + o, chips)
        return pltpu.make_async_remote_copy(
            src_ref=tcomb.at[s, to], dst_ref=trecv[s].at[chip], send_sem=ts_sem.at[s, o], recv_sem=tr_sem.at[s, o],
            device_id={"tm": 2 * to + core}, device_id_type=MESH,
        )

    pl.semaphore_wait(barrier, n - 1)
    for s in range(steps):
        across(s).start()

    @pl.loop(1, n)
    def _(o):
        hop(rsend, rrecv, rs_sem, rr_sem, o).start()

    for s in range(steps):
        across(s).wait_recv()
        theirs = plan_ref[s] == partner
        mix = jnp.where(theirs, tpart[s].astype(jnp.float32), tsend[s, core].astype(jnp.float32))
        tcomb[s] = mix.astype(jnp.bfloat16)
        trecv[s][chip] = tcomb[s, chip]

        @pl.loop(1, chips)
        def _(o):
            spread(s, lax.rem(o + chips // 2 - 1, chips - 1) + 1).start()

    @pl.loop(1, n)
    def _(o):
        hop(rsend, rrecv, rs_sem, rr_sem, o).wait_recv()

    for v in range(halves):
        for a in range(n):
            xs[v, a * own : (a + 1) * own, :] = rrecv[a, :, v * LANES : (v + 1) * LANES].astype(jnp.float32)
        xs[v, n * own :, :] = jnp.zeros((xs.shape[1] - n * own, LANES), jnp.float32)
    shift = lax.broadcasted_iota(jnp.int32, (LANES, width * LANES), 1) - lax.broadcasted_iota(
        jnp.int32, (LANES, width * LANES), 0
    )
    band = jnp.where((shift >= 0) & (shift < taps), 1.0, 0.0).astype(jnp.bfloat16)
    live = jnp.sum(mask_v[...].astype(jnp.float32), axis=1, keepdims=True)
    scale = jnp.sqrt(taps / (1.0 + live))

    def frame(i, carry):
        tiles = [
            xs[q % halves, pl.ds(i + (q // halves) * own, n, stride=own), :] for q in range(halves + width - 1)
        ]
        x = jnp.concatenate(
            [jnp.concatenate(tiles[h : h + width], axis=1) for h in range(halves)], axis=0
        )
        frames[i] = x.astype(jnp.bfloat16)
        sq = x * x
        high = sq.astype(jnp.bfloat16)
        low = (sq - high.astype(jnp.float32)).astype(jnp.bfloat16)
        energy = lax.dot_general(
            jnp.concatenate([high, low], axis=0), band, dims, preferred_element_type=jnp.float32
        )
        energy = energy[: halves * n] + energy[halves * n :]
        factor = scale * mask_s[i * n + me].astype(jnp.float32)
        inv[i] = factor / jnp.sqrt(energy + 1e-06)
        return carry

    lax.fori_loop(0, own, frame, 0, unroll=unroll)
    if width > 2:
        tmpl[:, 2 * LANES :] = jnp.zeros((rows, (width - 2) * LANES), jnp.float32)

    for s in range(steps):

        @pl.loop(1, chips)
        def _(o):
            spread(s, o).wait_recv()

        got = trecv[s][lax.div(plan_ref[s], 2)].astype(jnp.float32)
        tmpl[:, : 2 * LANES] = got
        energy = jnp.sum(got * got, axis=1, keepdims=True)
        wts[...] = jnp.broadcast_to(1.0 / jnp.sqrt(energy + 1e-06), (rows, LANES))
        acc[s] = jnp.zeros(acc.shape[1:], jnp.float32)

        def channel(i, carry):
            banks = []
            for k in range(kcount):
                base = jnp.broadcast_to(tmpl[pl.ds(k * own + i, 1), :], (16, width * LANES)).astype(jnp.bfloat16)
                base = jnp.concatenate([base] * (LANES // 16), axis=0)
                banks.append(pltpu.roll(base, 0, 1, stride=1, stride_axis=0))
            raw = lax.dot_general(
                frames[i], jnp.concatenate(banks, axis=0), dims, preferred_element_type=jnp.float32
            )
            norm = inv[i]
            for k in range(kcount):
                part = raw[:, k * LANES : (k + 1) * LANES] * norm * wts[pl.ds(k * own + i, 1), :]
                for h in range(halves):
                    at = (h * kcount + k) * n
                    acc[s, at : at + n, :] += part[h * n : (h + 1) * n]
            return carry

        lax.fori_loop(0, own, channel, 0, unroll=unroll)

        for d in range(n):
            osend[s, d] = acc[s, pl.ds(d, halves * kcount, stride=n), :]
        orecv[s, me] = osend[s, me]

        @pl.loop(1, n)
        def _(o):
            hop(osend.at[s], orecv.at[s], os_sem.at[s], or_sem.at[s], o).start()

    for s in range(steps):

        @pl.loop(1, n)
        def _(o):
            hop(osend.at[s], orecv.at[s], os_sem.at[s], or_sem.at[s], o).wait_recv()

        final = jnp.sum(orecv[s], axis=0)
        for h in range(halves):
            out_ref[s, :, h * LANES : (h + 1) * LANES] = final[h * kcount : (h + 1) * kcount]

    for s in range(steps):
        across(s).wait_send()

        @pl.loop(1, chips)
        def _(o):
            spread(s, o).wait_send()

        @pl.loop(1, n)
        def _(o):
            hop(osend.at[s], orecv.at[s], os_sem.at[s], or_sem.at[s], o).wait_send()

    @pl.loop(1, n)
    def _(o):
        hop(rsend, rrecv, rs_sem, rr_sem, o).wait_send()


def shards(records, bank, plan, template_ids, channel_mask):
    n = lax.axis_size("tm")
    steps, kcount = template_ids.shape
    chans, block = records.shape
    taps = bank.shape[2]
    own = chans // n
    rows = kcount * own
    halves = block // LANES
    width = up(LANES + taps - 1, LANES) // LANES
    vmem = pl.BlockSpec(memory_space=pltpu.VMEM)
    smem = pl.BlockSpec(memory_space=pltpu.SMEM)
    f32, bf16 = jnp.float32, jnp.bfloat16
    dma = pltpu.SemaphoreType.DMA
    extra = -(-(halves + width - 2) // halves)
    return pl.pallas_call(
        functools.partial(kernel, n, steps, kcount, taps, own),
        out_shape=jax.ShapeDtypeStruct((steps, kcount, block), f32),
        in_specs=[smem, smem, smem, vmem, vmem, pl.BlockSpec(memory_space=pl.ANY)],
        out_specs=vmem,
        scratch_shapes=[
            pltpu.VMEM((steps, 2, kcount * chans, LANES), f32),
            pltpu.VMEM((halves, chans, LANES), f32),
            pltpu.VMEM((steps, 2, n // 2, rows, 2 * LANES), bf16),
            pltpu.VMEM((steps, n // 2, rows, 2 * LANES), bf16),
            pltpu.VMEM((steps, n // 2, rows, 2 * LANES), bf16),
            pltpu.VMEM((n, own, block), bf16),
            [pltpu.VMEM((n // 2, rows, 2 * LANES), bf16)] * steps,
            pltpu.VMEM((n, own, block), bf16),
            pltpu.VMEM((halves, (n + extra) * own, LANES), f32),
            pltpu.VMEM((own, halves * n, width * LANES), bf16),
            pltpu.VMEM((own, halves * n, LANES), f32),
            pltpu.VMEM((rows, width * LANES), f32),
            pltpu.VMEM((rows, LANES), f32),
            pltpu.VMEM((steps, halves * kcount * n, LANES), f32),
            pltpu.VMEM((steps, n, halves * kcount, LANES), f32),
            pltpu.VMEM((steps, n, halves * kcount, LANES), f32),
            pltpu.VMEM(bank.shape, bf16),
            dma(()), dma((steps,)), dma((steps,)), dma((steps, n // 2)), dma((steps, n // 2)),
            dma((n,)), dma((n,)), dma((steps, n)), dma((steps, n)),
        ],
        compiler_params=pltpu.CompilerParams(
            collective_id=0, has_side_effects=True, vmem_limit_bytes=60 * 1024 * 1024
        ),
        name="detect",
    )(plan, template_ids.T, channel_mask, channel_mask.reshape(1, -1), records, bank)


def solution(mesh):
    placed = (
        P("groups", "tm"),
        P("tm", "groups", None),
        P("groups"),
        P("groups", None),
        P("groups"),
    )
    return jax.shard_map(
        shards, mesh=mesh, in_specs=placed, out_specs=P("groups", None, "tm"), check_vma=False
    )
```

profile of v0, /device:TPU:0, one launch (start us, length us, event | category | flops | bytes accessed | tf_op | source)
XLA Modules:
  0.0 27.3 jit_solution(14230827014548306768)
XLA Ops:
  0.0 26.0 %detect.1 = f32[3,2,256]{2,1,0:T(2,128)} custom-call(s32[3]{0:T(128)} %plan_ref.1, s32[2,3]{1,0:T(2,128)} %bitcast.3, s32[192]{0:T(256)} %mask_s.1, s32[1,192]{1,0:T(1,128)} %bitcast.2, bf16[192,256]{1,0:T(8,128)(2,1)} %rec_ref.1, bf16[16,192,240]{2,1,0:T(8,128)(2,1)} %bank_ref.1), custom_call_target="tpu_custom_call" | custom-call | tf_op jit(solution)/shard_map/detect/pallas_call | solution.py:224
  26.0 1.3 %copy.7 = f32[3,2,256]{2,1,0:T(2,128)} copy(f32[3,2,256]{2,1,0:T(2,128)} %detect.1) | data formatting | bytes 12288
where the time goes:
time: 27.5 us; the launch traced here: 27.3 us
  Pallas kernels  26 us (95%)
  local copies, waits for them, and re-layouts  1.29 us (5%)
    pallas_call x1, Pallas kernels, shards(): pl.pallas_call(functools.partial(kernel, n, steps, kcount, taps, own), ou...  26 us
    unnamed x1, local copies, waits for them, and re-layouts  1.29 us

commit v1 on v0

v1 whole, which is shorter than its diff:
```python
import functools

import jax
import jax.numpy as jnp
from jax import lax
from jax.experimental import pallas as pl
from jax.experimental.pallas import tpu as pltpu
from jax.sharding import PartitionSpec as P

MESH = pl.DeviceIdType.MESH
LANES = 128


def up(value, unit):
    return -(-value // unit) * unit


def kernel(
    n, steps, kk, taps,
    plan_in, ids_in, mask_in, row_in, rec_ref, bank_ref, out_ref,
    plan_ref, ids_ref, mask_s, mask_v, bank_v, tsend, tpart, tcomb, trecv, rrecv, xs, frames, inv, tmpl, wts, acc, osend, orecv,
    ready, few_sem, bank_sem, rs_sem, rr_sem, fs_sem, fr_sem, cs_sem, cr_sem, ts_sem, tr_sem, os_sem, or_sem,
):
    me = lax.axis_index("tm")
    chip, core = me // 2, me % 2
    chips = n // 2
    partner = me + 1 - 2 * core
    chans, block = rec_ref.shape
    own = chans // chips
    halves = block // LANES
    part = LANES // 2
    width = frames.shape[2] // LANES
    dims = (((1,), (1,)), ((), ()))

    def tell(sem, to):
        pl.semaphore_signal(sem, inc=1, device_id={"tm": to}, device_id_type=MESH)

    def push(src, dst, send_sem, recv_sem, to):
        return pltpu.make_async_remote_copy(
            src_ref=src, dst_ref=dst, send_sem=send_sem, recv_sem=recv_sem,
            device_id={"tm": to}, device_id_type=MESH,
        )

    barrier = pltpu.get_barrier_semaphore()
    tell(barrier, partner)

    @pl.loop(chip + 1, chips)
    def _(q):
        tell(barrier, 2 * q)
        tell(barrier, 2 * q + 1)

    fetch = pltpu.make_async_copy(bank_ref, bank_v, bank_sem)
    fetch.start()
    few = [
        pltpu.make_async_copy(src, dst, few_sem.at[i])
        for i, (src, dst) in enumerate([(plan_in, plan_ref), (ids_in, ids_ref), (mask_in, mask_s), (row_in, mask_v)])
    ]
    for copy in few:
        copy.start()
    pl.semaphore_wait(barrier, 1 + 2 * chip)

    @pl.loop(0, chip)
    def _(q):
        tell(ready.at[chip], 2 * q)
        tell(ready.at[chip], 2 * q + 1)

    def send_records(q):
        rows = pl.ds(pl.multiple_of(q * own, 8), own)
        return push(rec_ref.at[rows], rrecv.at[core, chip], rs_sem, rr_sem, 2 * q + core)

    def across(s):
        return push(tsend.at[s], tpart.at[s], cs_sem.at[s], cr_sem.at[s], partner)

    def spread(s, q):
        return push(tcomb.at[s, q], trecv[s].at[chip], ts_sem, tr_sem.at[s], 2 * q + core)

    @pl.loop(0, chip)
    def _(q):
        send_records(q).start()

    keep = pltpu.make_async_copy(
        rec_ref.at[pl.ds(pl.multiple_of(chip * own, 8), own)], rrecv.at[core, chip], bank_sem
    )
    for copy in few:
        copy.wait()
    fetch.wait()
    keep.start()
    for s in range(steps):
        for j in range(kk):
            pick = bank_v[ids_ref[(1 - core) * kk + j, s]]
            for q in range(chips):
                tsend[s, q, j] = pick[q * own : (q + 1) * own]
        across(s).start()
    for s in range(steps):
        theirs = plan_ref[s] == partner
        across(s).wait_recv()
        for j in range(kk):
            pick = bank_v[ids_ref[core * kk + j, s]]
            for q in range(chips):
                tcomb[s, q, j] = jnp.where(theirs, tpart[s, q, j], pick[q * own : (q + 1) * own])
        trecv[s][chip] = tcomb[s, chip]

        @pl.loop(0, chip)
        def _(q):
            spread(s, q).start()

    @pl.loop(chip + 1, chips)
    def _(q):
        pl.semaphore_wait(ready.at[q], 2)
        send_records(q).start()
        spread(0, q).start()

    for s in range(1, steps):

        @pl.loop(chip + 1, chips)
        def _(q):
            spread(s, q).start()

    keep.wait()
    others = pl.ds(0, chips - 1)
    got_records = push(rrecv.at[0, others], rrecv.at[0, others], rs_sem, rr_sem, partner)
    got_records.wait_recv()
    forward = push(rrecv.at[core], rrecv.at[core], fs_sem, fr_sem, partner)
    forward.start()
    forward.wait_recv()

    for v in range(halves):
        for a in range(n):
            xs[v, a * own : (a + 1) * own, :] = rrecv[a % 2, a // 2, :, v * LANES : (v + 1) * LANES].astype(jnp.float32)
        xs[v, n * own :, :] = jnp.zeros((xs.shape[1] - n * own, LANES), jnp.float32)
    shift = lax.broadcasted_iota(jnp.int32, (part, width * LANES), 1) - lax.broadcasted_iota(
        jnp.int32, (part, width * LANES), 0
    )
    band = jnp.where((shift >= 0) & (shift < taps), 1.0, 0.0).astype(jnp.bfloat16)
    live = jnp.sum(mask_v[...].astype(jnp.float32), axis=1, keepdims=True)
    scale = jnp.sqrt(taps / (1.0 + live))
    left = lax.broadcasted_iota(jnp.int32, (n, LANES), 1) < part

    def frame(i, carry):
        tiles = [
            xs[q % halves, pl.ds(i + (q // halves) * own, n, stride=own), :] for q in range(halves + width)
        ]
        turned = [pltpu.roll(tile, part, 1) for tile in tiles]
        odd = [jnp.where(left, turned[q], turned[q + 1]) for q in range(halves + width - 1)]
        x = jnp.concatenate(
            [jnp.concatenate(some[h : h + width], axis=1) for some in (tiles, odd) for h in range(halves)], axis=0
        )
        frames[i] = x.astype(jnp.bfloat16)
        sq = x * x
        high = sq.astype(jnp.bfloat16)
        low = (sq - high.astype(jnp.float32)).astype(jnp.bfloat16)
        energy = lax.dot_general(
            jnp.concatenate([high, low], axis=0), band, dims, preferred_element_type=jnp.float32
        )
        energy = energy[: 2 * halves * n] + energy[2 * halves * n :]
        factor = scale * mask_s[chip * own + i].astype(jnp.float32)
        inv[i] = factor / jnp.sqrt(energy + 1e-06)
        return carry

    lax.fori_loop(0, own, frame, 0, unroll=own)

    for s in range(steps):
        some = trecv[s].at[others]
        push(some, some, ts_sem, tr_sem.at[s], partner).wait_recv()
        for j in range(kk):
            got = trecv[s][lax.div(plan_ref[s], 2), j].astype(jnp.float32)
            tmpl[...] = jnp.concatenate([got, jnp.zeros((own, width * LANES - taps), jnp.float32)], axis=1)
            energy = jnp.sum(got * got, axis=1, keepdims=True)
            wts[...] = jnp.broadcast_to(1.0 / jnp.sqrt(energy + 1e-06), (own, part))

            def channel(i, total):
                base = jnp.broadcast_to(tmpl[pl.ds(i, 1), :], (16, width * LANES)).astype(jnp.bfloat16)
                base = jnp.concatenate([base] * (part // 16), axis=0)
                taps_of = pltpu.roll(base, 0, 1, stride=1, stride_axis=0)
                raw = lax.dot_general(frames[i], taps_of, dims, preferred_element_type=jnp.float32)
                return total + raw * inv[i] * wts[pl.ds(i, 1), :]

            total = lax.fori_loop(0, own, channel, jnp.zeros((2 * halves * n, part), jnp.float32), unroll=own)
            total = jnp.concatenate([total[: halves * n], total[halves * n :]], axis=1)
            at = (s * kk + j) * halves * n
            acc[at : at + halves * n, :] = total

    rows = steps * kk * halves
    for d in range(n):
        osend[d] = acc[pl.ds(d, rows, stride=n), :]
    orecv[me] = osend[me]

    def give(d):
        return push(osend.at[d], orecv.at[me], os_sem, or_sem, d)

    @pl.loop(0, me)
    def _(d):
        give(d).start()

    @pl.loop(me + 1, n)
    def _(d):
        give(d).start()

    sums = orecv.at[pl.ds(0, n - 1)]
    push(sums, sums, os_sem, or_sem, partner).wait_recv()
    totals = jnp.sum(orecv[...].reshape(chips, 2, rows, LANES), axis=0)
    for c in range(2):
        final = totals[c]
        for s in range(steps):
            for j in range(kk):
                for h in range(halves):
                    r = (s * kk + j) * halves + h
                    out_ref[s, c * kk + j, h * LANES : (h + 1) * LANES] = final[r]

    got_records.wait_send()
    forward.wait_send()
    for s in range(steps):
        across(s).wait_send()
    some = tcomb.at[:, others]
    push(some, some, ts_sem, tr_sem.at[0], partner).wait_send()
    push(sums, sums, os_sem, or_sem, partner).wait_send()


def shards(records, bank, plan, template_ids, channel_mask):
    n = lax.axis_size("tm")
    chips = n // 2
    steps, kcount = template_ids.shape
    chans, block = records.shape
    slots, _, taps = bank.shape
    kk = kcount // 2
    own = up(chans // chips, 8)
    if own * chips != chans:
        few = chans // chips
        more = own - few
        records = jnp.pad(records.reshape(chips, few, block), ((0, 0), (0, more), (0, 0))).reshape(-1, block)
        bank = jnp.pad(bank.reshape(slots, chips, few, taps), ((0, 0), (0, 0), (0, more), (0, 0))).reshape(slots, -1, taps)
        channel_mask = jnp.pad(channel_mask.reshape(chips, few), ((0, 0), (0, more))).reshape(-1)
    halves = block // LANES
    part = LANES // 2
    width = up(part + taps - 1, LANES) // LANES
    vmem = pl.BlockSpec(memory_space=pltpu.VMEM)
    hbm = pl.BlockSpec(memory_space=pl.ANY)
    f32, bf16 = jnp.float32, jnp.bfloat16
    dma = pltpu.SemaphoreType.DMA
    extra = -(-(halves + width - 1) // halves)
    rows = steps * kk * halves
    return pl.pallas_call(
        functools.partial(kernel, n, steps, kk, taps),
        out_shape=jax.ShapeDtypeStruct((steps, kcount, block), f32),
        in_specs=[hbm] * 6,
        out_specs=vmem,
        scratch_shapes=[
            pltpu.SMEM((steps,), jnp.int32),
            pltpu.SMEM((kcount, steps), jnp.int32),
            pltpu.SMEM(channel_mask.shape, jnp.int32),
            pltpu.VMEM((1, channel_mask.shape[0]), jnp.int32),
            pltpu.VMEM(bank.shape, bf16),
            pltpu.VMEM((steps, chips, kk, own, taps), bf16),
            pltpu.VMEM((steps, chips, kk, own, taps), bf16),
            pltpu.VMEM((steps, chips, kk, own, taps), bf16),
            [pltpu.VMEM((chips, kk, own, taps), bf16)] * steps,
            pltpu.VMEM((2, chips, own, block), bf16),
            pltpu.VMEM((halves, (n + extra) * own, LANES), f32),
            pltpu.VMEM((own, 2 * halves * n, width * LANES), bf16),
            pltpu.VMEM((own, 2 * halves * n, part), f32),
            pltpu.VMEM((own, width * LANES), f32),
            pltpu.VMEM((own, part), f32),
            pltpu.VMEM((rows * n, LANES), f32),
            pltpu.VMEM((n, rows, LANES), f32),
            pltpu.VMEM((n, rows, LANES), f32),
            pltpu.SemaphoreType.REGULAR((chips,)),
            dma((4,)), dma(()), dma(()), dma(()), dma(()), dma(()), dma((steps,)), dma((steps,)), dma(()), dma((steps,)),
            dma(()), dma(()),
        ],
        compiler_params=pltpu.CompilerParams(
            collective_id=0, has_side_effects=True, vmem_limit_bytes=60 * 1024 * 1024
        ),
        name="detect",
    )(plan, template_ids.T, channel_mask, channel_mask.reshape(1, -1), records, bank)


def solution(mesh):
    placed = (
        P("groups", "tm"),
        P("tm", "groups", None),
        P("groups"),
        P("groups", None),
        P("groups"),
    )
    return jax.shard_map(
        shards, mesh=mesh, in_specs=placed, out_specs=P("groups", None, "tm"), check_vma=False
    )
```

time: 27.5 us -> 23.9 us (0.87)
  Pallas kernels: 26 us -> 22.3 us
    pallas_call x1, Pallas kernels: 26 us -> 22.3 us  [shards(): pl.pallas_call(functools.partial(kernel, n, steps, kk, taps), out_shape=j...]
where the time goes in v1:
time: 23.9 us; the launch traced here: 23.6 us
  Pallas kernels  22.3 us (93%)
  local copies, waits for them, and re-layouts  1.29 us (5%)
    pallas_call x1, Pallas kernels, shards(): pl.pallas_call(functools.partial(kernel, n, steps, kk, taps), out_shape=j...  22.3 us
    unnamed x1, local copies, waits for them, and re-layouts  1.29 us

profile of v1, /device:TPU:0, one launch (start us, length us, event | category | flops | bytes accessed | tf_op | source)
XLA Modules:
  0.0 23.6 jit_solution(15533049358565659004)
XLA Ops:
  0.0 22.3 %detect.1 = f32[3,2,256]{2,1,0:T(2,128)} custom-call(s32[3]{0:T(128)} %plan_in.1, s32[2,3]{1,0:T(2,128)} %bitcast.3, s32[192]{0:T(256)} %mask_in.1, s32[1,192]{1,0:T(1,128)} %bitcast.2, bf16[192,256]{1,0:T(8,128)(2,1)} %rec_ref.1, bf16[16,192,240]{2,1,0:T(8,128)(2,1)} %bank_ref.1), custom_call_target="tpu_custom_call" | custom-call | tf_op jit(solution)/shard_map/detect/pallas_call | solution.py:242
  22.4 1.3 %copy.7 = f32[3,2,256]{2,1,0:T(2,128)} copy(f32[3,2,256]{2,1,0:T(2,128)} %detect.1) | data formatting | bytes 12288

commit v2 on v1

v2 whole, which is shorter than its diff:
```python
import functools

import jax
import jax.numpy as jnp
from jax import lax
from jax.experimental import pallas as pl
from jax.experimental.pallas import tpu as pltpu
from jax.sharding import PartitionSpec as P

MESH = pl.DeviceIdType.MESH
LANES = 128
DIRECT = 0


def up(value, unit):
    return -(-value // unit) * unit


def kernel(
    n, owners, steps, kk, taps,
    plan_in, ids_in, mask_in, row_in, rec_ref, bank_ref, out_ref,
    plan_ref, ids_ref, mask_s, mask_v, bank_v, tsend, tpart, tcomb, pair_in, pair_out, trecv, tpair, rrecv,
    xs, frames, inv, tmpl, wts, acc, osend, orecv,
    ready, few_sem, bank_sem, rs_sem, rr_sem, fs_sem, fr_sem, cs_sem, cr_sem, ps_sem, pr_sem, ts_sem, tr_sem,
    qs_sem, qr_sem, os_sem, or_sem,
):
    me = lax.axis_index("tm")
    chip, core = me // 2, me % 2
    chips = n // 2
    partner = me + 1 - 2 * core
    side = chip % 2
    twin = chip + 1 - 2 * side
    chans, block = rec_ref.shape
    own = chans // owners
    halves = block // LANES
    part = LANES // 2
    width = frames.shape[2] // LANES
    dims = (((1,), (1,)), ((), ()))
    direct = min(DIRECT, steps)
    paired = range(direct, steps)
    owner = chip < owners

    def tell(sem, to):
        pl.semaphore_signal(sem, inc=1, device_id={"tm": to}, device_id_type=MESH)

    def push(src, dst, send_sem, recv_sem, to):
        return pltpu.make_async_remote_copy(
            src_ref=src, dst_ref=dst, send_sem=send_sem, recv_sem=recv_sem,
            device_id={"tm": to}, device_id_type=MESH,
        )

    def sent(ref, sem):
        push(ref, ref, sem, sem, partner).wait_send()

    def landed(ref, sem):
        push(ref, ref, sem, sem, partner).wait_recv()

    fetch = pltpu.make_async_copy(bank_ref, bank_v, bank_sem)
    fetch.start()
    few = [
        pltpu.make_async_copy(src, dst, few_sem.at[i])
        for i, (src, dst) in enumerate([(plan_in, plan_ref), (ids_in, ids_ref), (mask_in, mask_s), (row_in, mask_v)])
    ]
    for copy in few:
        copy.start()
    barrier = pltpu.get_barrier_semaphore()
    tell(barrier, partner)

    @pl.loop(chip + 1, chips)
    def _(q):
        tell(barrier, 2 * q + core)

    pl.semaphore_wait(barrier, 1 + chip)
    lower = jnp.minimum(chip, owners)

    def rows_of(q):
        return rec_ref.at[pl.ds(pl.multiple_of(q * own, 8), own)]

    def send_records(q):
        return push(rows_of(q), rrecv.at[core, chip], rs_sem, rr_sem, 2 * q + core)

    def across(s):
        return push(tsend.at[s], tpart.at[s], cs_sem.at[s], cr_sem.at[s], partner)

    def spread(s, q):
        return push(tcomb.at[s, q % 2, q // 2], trecv[s].at[chip], ts_sem.at[s], tr_sem.at[s], 2 * q + core)

    def to_twin(s):
        at = s - direct
        return push(tcomb.at[s, 1 - side], pair_in.at[at], ps_sem.at[at], pr_sem.at[at], 2 * twin + core)

    def spread_pair(s, i):
        at = s - direct
        return push(
            pair_out.at[at, i], tpair[at].at[chip // 2], qs_sem.at[at], qr_sem.at[at], 2 * (2 * i + side) + core
        )

    for copy in few:
        copy.wait()
    fetch.wait()
    order = list(paired) + list(range(direct))
    for s in order:
        for j in range(kk):
            pick = bank_v[ids_ref[(1 - core) * kk + j, s]]
            for q in range(owners):
                tsend[s, q % 2, q // 2, j] = pick[q * own : (q + 1) * own]
        across(s).start()

    @pl.loop(0, chip)
    def _(q):
        tell(ready.at[chip], 2 * q + core)

    @pl.loop(0, lower)
    def _(q):
        send_records(q).start()

    for s in order:
        theirs = plan_ref[s] == partner
        across(s).wait_recv()
        for j in range(kk):
            pick = bank_v[ids_ref[core * kk + j, s]]
            for q in range(owners):
                at = (s, q % 2, q // 2, j)
                tcomb[at] = jnp.where(theirs, tpart[at], pick[q * own : (q + 1) * own])
        if s >= direct:
            if s == direct:

                @pl.when(twin > chip)
                def _():
                    pl.semaphore_wait(ready.at[twin], 1)

            to_twin(s).start()
        else:

            @pl.loop(0, lower)
            def _(q):
                spread(s, q).start()

    keep = pltpu.make_async_copy(rows_of(lax.rem(chip, owners)), rrecv.at[core, chip], bank_sem)
    keep.start()

    @pl.loop(chip + 1, owners)
    def _(q):
        @pl.when(q != twin)
        def _():
            pl.semaphore_wait(ready.at[q], 1)

        send_records(q).start()
        if direct:
            spread(0, q).start()

    for s in range(1, direct):

        @pl.loop(chip + 1, owners)
        def _(q):
            spread(s, q).start()

    for s in paired:
        at = s - direct
        landed(pair_in.at[at], pr_sem.at[at])
        theirs = lax.div(plan_ref[s], 2) == twin
        for i in range(owners // 2):
            pair_out[at, i] = jnp.where(theirs, pair_in[at, i], tcomb[s, side, i])

        @pl.loop(0, owners // 2)
        def _(i):
            @pl.when(i != chip // 2)
            def _():
                spread_pair(s, i).start()

    keep.wait()
    rows = steps * kk * halves
    others = pl.ds(0, chips - 1)

    @pl.when(owner)
    def _():
        for s in paired:
            tpair[s - direct][chip // 2] = pair_out[s - direct, lax.rem(chip // 2, owners // 2)]
        for s in range(direct):
            trecv[s][chip] = tcomb[s, side, lax.rem(chip // 2, owners // 2)]
        landed(rrecv.at[0, others], rr_sem)
        forward = push(rrecv.at[core], rrecv.at[core], fs_sem, fr_sem, partner)
        forward.start()
        forward.wait_recv()

        for v in range(halves):
            for a in range(n):
                xs[v, a * own : (a + 1) * own, :] = rrecv[a % 2, a // 2, :, v * LANES : (v + 1) * LANES].astype(
                    jnp.float32
                )
            xs[v, n * own :, :] = jnp.zeros((xs.shape[1] - n * own, LANES), jnp.float32)
        shift = lax.broadcasted_iota(jnp.int32, (part, width * LANES), 1) - lax.broadcasted_iota(
            jnp.int32, (part, width * LANES), 0
        )
        band = jnp.where((shift >= 0) & (shift < taps), 1.0, 0.0).astype(jnp.bfloat16)
        live = jnp.sum(mask_v[...].astype(jnp.float32), axis=1, keepdims=True)
        scale = jnp.sqrt(taps / (1.0 + live))
        left = lax.broadcasted_iota(jnp.int32, (n, LANES), 1) < part

        def frame(i, carry):
            tiles = [
                xs[q % halves, pl.ds(i + (q // halves) * own, n, stride=own), :] for q in range(halves + width)
            ]
            turned = [pltpu.roll(tile, part, 1) for tile in tiles]
            odd = [jnp.where(left, turned[q], turned[q + 1]) for q in range(halves + width - 1)]
            x = jnp.concatenate(
                [jnp.concatenate(some[h : h + width], axis=1) for some in (tiles, odd) for h in range(halves)], axis=0
            )
            frames[i] = x.astype(jnp.bfloat16)
            sq = x * x
            high = sq.astype(jnp.bfloat16)
            low = (sq - high.astype(jnp.float32)).astype(jnp.bfloat16)
            energy = lax.dot_general(
                jnp.concatenate([high, low], axis=0), band, dims, preferred_element_type=jnp.float32
            )
            energy = energy[: 2 * halves * n] + energy[2 * halves * n :]
            factor = scale * mask_s[chip * own + i].astype(jnp.float32)
            inv[i] = factor / jnp.sqrt(energy + 1e-06)
            return carry

        lax.fori_loop(0, own, frame, 0, unroll=own)

        for s in range(steps):
            if s >= direct:
                landed(tpair[s - direct].at[pl.ds(0, chips // 2 - 1)], qr_sem.at[s - direct])
            else:
                landed(trecv[s].at[others], tr_sem.at[s])
            for j in range(kk):
                if s >= direct:
                    got = tpair[s - direct][lax.div(plan_ref[s], 4), j]
                else:
                    got = trecv[s][lax.div(plan_ref[s], 2), j]
                got = got.astype(jnp.float32)
                tmpl[...] = jnp.concatenate([got, jnp.zeros((own, width * LANES - taps), jnp.float32)], axis=1)
                energy = jnp.sum(got * got, axis=1, keepdims=True)
                wts[...] = jnp.broadcast_to(1.0 / jnp.sqrt(energy + 1e-06), (own, part))

                def channel(i, total):
                    base = jnp.broadcast_to(tmpl[pl.ds(i, 1), :], (16, width * LANES)).astype(jnp.bfloat16)
                    base = jnp.concatenate([base] * (part // 16), axis=0)
                    taps_of = pltpu.roll(base, 0, 1, stride=1, stride_axis=0)
                    raw = lax.dot_general(frames[i], taps_of, dims, preferred_element_type=jnp.float32)
                    return total + raw * inv[i] * wts[pl.ds(i, 1), :]

                total = lax.fori_loop(0, own, channel, jnp.zeros((2 * halves * n, part), jnp.float32), unroll=own)
                total = jnp.concatenate([total[: halves * n], total[halves * n :]], axis=1)
                at = (s * kk + j) * halves * n
                acc[at : at + halves * n, :] = total

        for d in range(n):
            osend[d] = acc[pl.ds(d, rows, stride=n), :]
        orecv[me] = osend[me]

        @pl.loop(jnp.maximum(chip + 1, owners), chips)
        def _(q):
            @pl.when(q != twin)
            def _():
                pl.semaphore_wait(ready.at[q], 1)

        def give(d):
            return push(osend.at[d], orecv.at[me], os_sem, or_sem, d)

        @pl.loop(0, me)
        def _(d):
            give(d).start()

        @pl.loop(me + 1, n)
        def _(d):
            give(d).start()

        landed(orecv.at[pl.ds(0, 2 * owners - 1)], or_sem)

    @pl.when(jnp.logical_not(owner))
    def _():
        @pl.loop(chip + 1, chips)
        def _(q):
            @pl.when(q != twin)
            def _():
                pl.semaphore_wait(ready.at[q], 1)

        landed(orecv, or_sem)

    totals = jnp.sum(orecv[...].reshape(owners, 2, rows, LANES), axis=0)
    for c in range(2):
        for s in range(steps):
            for j in range(kk):
                for h in range(halves):
                    r = (s * kk + j) * halves + h
                    out_ref[s, c * kk + j, h * LANES : (h + 1) * LANES] = totals[c, r]

    for s in range(steps):
        across(s).wait_send()
    for s in paired:
        to_twin(s).wait_send()

    @pl.when(owner)
    def _():
        sent(rrecv.at[0, pl.ds(0, owners - 1)], rs_sem)
        push(rrecv.at[core], rrecv.at[core], fs_sem, fr_sem, partner).wait_send()
        sent(osend.at[pl.ds(0, n - 1)], os_sem)
        for s in paired:
            sent(pair_out.at[s - direct, pl.ds(0, owners // 2 - 1)], qs_sem.at[s - direct])
        for s in range(direct):
            sent(trecv[s].at[pl.ds(0, owners - 1)], ts_sem.at[s])

    @pl.when(jnp.logical_not(owner))
    def _():
        sent(rrecv.at[0, pl.ds(0, owners)], rs_sem)
        for s in paired:
            sent(pair_out.at[s - direct], qs_sem.at[s - direct])
        for s in range(direct):
            sent(trecv[s].at[pl.ds(0, owners)], ts_sem.at[s])


def shards(records, bank, plan, template_ids, channel_mask):
    n = lax.axis_size("tm")
    chips = n // 2
    owners = chips
    steps, kcount = template_ids.shape
    chans, block = records.shape
    slots, _, taps = bank.shape
    kk = kcount // 2
    own = up(-(-chans // owners), 8)
    if own * owners != chans:
        more = own * owners - chans
        records = jnp.pad(records, ((0, more), (0, 0)))
        bank = jnp.pad(bank, ((0, 0), (0, more), (0, 0)))
        channel_mask = jnp.pad(channel_mask, (0, more))
    halves = block // LANES
    part = LANES // 2
    width = up(part + taps - 1, LANES) // LANES
    vmem = pl.BlockSpec(memory_space=pltpu.VMEM)
    hbm = pl.BlockSpec(memory_space=pl.ANY)
    f32, bf16 = jnp.float32, jnp.bfloat16
    dma = pltpu.SemaphoreType.DMA
    extra = -(-(halves + width - 1) // halves)
    rows = steps * kk * halves
    piece = (kk, own, taps)
    direct = min(DIRECT, steps)
    return pl.pallas_call(
        functools.partial(kernel, n, owners, steps, kk, taps),
        out_shape=jax.ShapeDtypeStruct((steps, kcount, block), f32),
        in_specs=[hbm] * 6,
        out_specs=vmem,
        scratch_shapes=[
            pltpu.SMEM((steps,), jnp.int32),
            pltpu.SMEM((kcount, steps), jnp.int32),
            pltpu.SMEM(channel_mask.shape, jnp.int32),
            pltpu.VMEM((1, channel_mask.shape[0]), jnp.int32),
            pltpu.VMEM(bank.shape, bf16),
            pltpu.VMEM((steps, 2, owners // 2, *piece), bf16),
            pltpu.VMEM((steps, 2, owners // 2, *piece), bf16),
            pltpu.VMEM((steps, 2, owners // 2, *piece), bf16),
            pltpu.VMEM((max(steps - direct, 1), owners // 2, *piece), bf16),
            pltpu.VMEM((max(steps - direct, 1), owners // 2, *piece), bf16),
            [pltpu.VMEM((chips, *piece), bf16)] * direct,
            [pltpu.VMEM((chips // 2, *piece), bf16)] * (steps - direct),
            pltpu.VMEM((2, chips, own, block), bf16),
            pltpu.VMEM((halves, (n + extra) * own, LANES), f32),
            pltpu.VMEM((own, 2 * halves * n, width * LANES), bf16),
            pltpu.VMEM((own, 2 * halves * n, part), f32),
            pltpu.VMEM((own, width * LANES), f32),
            pltpu.VMEM((own, part), f32),
            pltpu.VMEM((rows * n, LANES), f32),
            pltpu.VMEM((n, rows, LANES), f32),
            pltpu.VMEM((2 * owners, rows, LANES), f32),
            pltpu.SemaphoreType.REGULAR((chips,)),
            dma((4,)), dma(()), dma(()), dma(()), dma(()), dma(()), dma((steps,)), dma((steps,)), dma((max(steps - direct, 1),)), dma((max(steps - direct, 1),)),
            dma((max(direct, 1),)), dma((max(direct, 1),)), dma((max(steps - direct, 1),)), dma((max(steps - direct, 1),)), dma(()), dma(()),
        ],
        compiler_params=pltpu.CompilerParams(
            collective_id=0, has_side_effects=True, vmem_limit_bytes=60 * 1024 * 1024
        ),
        name="detect",
    )(plan, template_ids.T, channel_mask, channel_mask.reshape(1, -1), records, bank)


def solution(mesh):
    placed = (
        P("groups", "tm"),
        P("tm", "groups", None),
        P("groups"),
        P("groups", None),
        P("groups"),
    )
    return jax.shard_map(
        shards, mesh=mesh, in_specs=placed, out_specs=P("groups", None, "tm"), check_vma=False
    )
```

time: 23.9 us -> 22.4 us (0.937)
  Pallas kernels: 22.3 us -> 20.9 us
    pallas_call x1, Pallas kernels: 22.3 us -> 20.9 us  [shards(): pl.pallas_call(functools.partial(kernel, n, owners, steps, kk, taps), out...]
where the time goes in v2:
time: 22.4 us; the launch traced here: 22.2 us
  Pallas kernels  20.9 us (93%)
  local copies, waits for them, and re-layouts  1.29 us (6%)
    pallas_call x1, Pallas kernels, shards(): pl.pallas_call(functools.partial(kernel, n, owners, steps, kk, taps), out...  20.9 us
    unnamed x1, local copies, waits for them, and re-layouts  1.29 us

profile of v2, /device:TPU:0, one launch (start us, length us, event | category | flops | bytes accessed | tf_op | source)
XLA Modules:
  0.0 22.2 jit_solution(15459887832373484829)
XLA Ops:
  0.0 20.9 %detect.1 = f32[3,2,256]{2,1,0:T(2,128)} custom-call(s32[3]{0:T(128)} %plan_in.1, s32[2,3]{1,0:T(2,128)} %bitcast.3, s32[192]{0:T(256)} %mask_in.1, s32[1,192]{1,0:T(1,128)} %bitcast.2, bf16[192,256]{1,0:T(8,128)(2,1)} %rec_ref.1, bf16[16,192,240]{2,1,0:T(8,128)(2,1)} %bank_ref.1), custom_call_target="tpu_custom_call" | custom-call | tf_op jit(solution)/shard_map/detect/pallas_call | solution.py:340
  20.9 1.3 %copy.7 = f32[3,2,256]{2,1,0:T(2,128)} copy(f32[3,2,256]{2,1,0:T(2,128)} %detect.1) | data formatting | bytes 12288

commit v3 on v1

v3 whole, which is shorter than its diff:
```python
import functools

import jax
import jax.numpy as jnp
from jax import lax
from jax.experimental import pallas as pl
from jax.experimental.pallas import tpu as pltpu
from jax.sharding import PartitionSpec as P

MESH = pl.DeviceIdType.MESH
LANES = 128
ALONG = (1, 0, 0)
ORDER = (0, 1, 2)


def up(value, unit):
    return -(-value // unit) * unit


def kernel(
    n, steps, kk, taps,
    plan_in, ids_in, mask_in, row_in, rec_ref, bank_ref, out_ref,
    plan_ref, ids_ref, mask_s, mask_v, bank_v, tsend, tpart, tcomb, pair_in, pair_out, tpair, rrecv,
    xs, frames, inv, tmpl, wts, acc, osend, orecv,
    ready, few_sem, bank_sem, rs_sem, rr_sem, fs_sem, fr_sem, cs_sem, cr_sem, ps_sem, pr_sem,
    qs_sem, qr_sem, os_sem, or_sem,
):
    me = lax.axis_index("tm")
    chip, core = me // 2, me % 2
    chips = n // 2
    partner = me + 1 - 2 * core
    chans, block = rec_ref.shape
    own = chans // chips
    halves = block // LANES
    part = LANES // 2
    width = frames.shape[2] // LANES
    dims = (((1,), (1,)), ((), ()))
    along = [ALONG[s % len(ALONG)] for s in range(steps)]
    order = sorted(range(steps), key=lambda s: ORDER[s % len(ORDER)])

    def side(s, q):
        return q // (1 + along[s]) % 2

    def place(s, q):
        return q // 4 * 2 + q % 2 if along[s] else q // 2

    def chip_at(s, i):
        return i // 2 * 4 + side(s, chip) * 2 + i % 2 if along[s] else i * 2 + side(s, chip)

    def twin(s):
        return chip + (1 - 2 * side(s, chip)) * (1 + along[s])


    def tell(sem, to):
        pl.semaphore_signal(sem, inc=1, device_id={"tm": to}, device_id_type=MESH)

    def push(src, dst, send_sem, recv_sem, to):
        return pltpu.make_async_remote_copy(
            src_ref=src, dst_ref=dst, send_sem=send_sem, recv_sem=recv_sem,
            device_id={"tm": to}, device_id_type=MESH,
        )

    def sent(ref, sem):
        push(ref, ref, sem, sem, partner).wait_send()

    def landed(ref, sem):
        push(ref, ref, sem, sem, partner).wait_recv()

    fetch = pltpu.make_async_copy(bank_ref, bank_v, bank_sem)
    fetch.start()
    few = [
        pltpu.make_async_copy(src, dst, few_sem.at[i])
        for i, (src, dst) in enumerate([(plan_in, plan_ref), (ids_in, ids_ref), (mask_in, mask_s), (row_in, mask_v)])
    ]
    for copy in few:
        copy.start()
    barrier = pltpu.get_barrier_semaphore()
    tell(barrier, partner)

    @pl.loop(chip + 1, chips)
    def _(q):
        tell(barrier, 2 * q + core)

    pl.semaphore_wait(barrier, 1 + chip)
    def rows_of(q):
        return rec_ref.at[pl.ds(pl.multiple_of(q * own, 8), own)]

    def send_records(q):
        return push(rows_of(q), rrecv.at[core, chip], rs_sem, rr_sem, 2 * q + core)

    def across(s):
        return push(tsend.at[s], tpart.at[s], cs_sem.at[s], cr_sem.at[s], partner)

    def to_twin(s):
        return push(tcomb.at[s, 1 - side(s, chip)], pair_in.at[s], ps_sem.at[s], pr_sem.at[s], 2 * twin(s) + core)

    def spread(s, i):
        return push(
            pair_out.at[s, i], tpair[s].at[place(s, chip)], qs_sem.at[s], qr_sem.at[s], 2 * chip_at(s, i) + core
        )

    for copy in few:
        copy.wait()
    fetch.wait()
    for s in order:
        for j in range(kk):
            pick = bank_v[ids_ref[(1 - core) * kk + j, s]]
            for q in range(chips):
                tsend[s, side(s, q), place(s, q), j] = pick[q * own : (q + 1) * own]
        across(s).start()

    @pl.loop(0, chip)
    def _(q):
        tell(ready.at[chip], 2 * q + core)

    @pl.loop(0, chip)
    def _(q):
        send_records(q).start()

    for s in order:
        theirs = plan_ref[s] == partner
        across(s).wait_recv()
        for j in range(kk):
            pick = bank_v[ids_ref[core * kk + j, s]]
            for q in range(chips):
                at = (s, side(s, q), place(s, q), j)
                tcomb[at] = jnp.where(theirs, tpart[at], pick[q * own : (q + 1) * own])
        if s == min(order, key=lambda t: (along[t] != along[s], order.index(t))):

            @pl.when(twin(s) > chip)
            def _():
                pl.semaphore_wait(ready.at[twin(s)], 1)

        to_twin(s).start()

    keep = pltpu.make_async_copy(rows_of(chip), rrecv.at[core, chip], bank_sem)
    keep.start()

    met = [order[0]] + [s for s in order if along[s] != along[order[0]]][:1]

    @pl.loop(chip + 1, chips)
    def _(q):
        fresh = functools.reduce(jnp.logical_and, [q != twin(s) for s in met])

        @pl.when(fresh)
        def _():
            pl.semaphore_wait(ready.at[q], 1)

        send_records(q).start()

    for s in order:
        landed(pair_in.at[s], pr_sem.at[s])
        theirs = lax.div(plan_ref[s], 2) == twin(s)
        for i in range(chips // 2):
            pair_out[s, i] = jnp.where(theirs, pair_in[s, i], tcomb[s, side(s, chip), i])

        @pl.loop(0, chips // 2)
        def _(i):
            @pl.when(i != place(s, chip))
            def _():
                spread(s, i).start()

    keep.wait()
    rows = steps * kk * halves
    others = pl.ds(0, chips - 1)

    for s in range(steps):
        tpair[s][place(s, chip)] = pair_out[s, place(s, chip)]
    landed(rrecv.at[0, others], rr_sem)
    forward = push(rrecv.at[core], rrecv.at[core], fs_sem, fr_sem, partner)
    forward.start()
    forward.wait_recv()

    for v in range(halves):
        for a in range(n):
            xs[v, a * own : (a + 1) * own, :] = rrecv[a % 2, a // 2, :, v * LANES : (v + 1) * LANES].astype(
                jnp.float32
            )
        xs[v, n * own :, :] = jnp.zeros((xs.shape[1] - n * own, LANES), jnp.float32)
    shift = lax.broadcasted_iota(jnp.int32, (part, width * LANES), 1) - lax.broadcasted_iota(
        jnp.int32, (part, width * LANES), 0
    )
    band = jnp.where((shift >= 0) & (shift < taps), 1.0, 0.0).astype(jnp.bfloat16)
    live = jnp.sum(mask_v[...].astype(jnp.float32), axis=1, keepdims=True)
    scale = jnp.sqrt(taps / (1.0 + live))
    left = lax.broadcasted_iota(jnp.int32, (n, LANES), 1) < part

    def frame(i, carry):
        tiles = [
            xs[q % halves, pl.ds(i + (q // halves) * own, n, stride=own), :] for q in range(halves + width)
        ]
        turned = [pltpu.roll(tile, part, 1) for tile in tiles]
        odd = [jnp.where(left, turned[q], turned[q + 1]) for q in range(halves + width - 1)]
        x = jnp.concatenate(
            [jnp.concatenate(some[h : h + width], axis=1) for some in (tiles, odd) for h in range(halves)], axis=0
        )
        frames[i] = x.astype(jnp.bfloat16)
        sq = x * x
        high = sq.astype(jnp.bfloat16)
        low = (sq - high.astype(jnp.float32)).astype(jnp.bfloat16)
        energy = lax.dot_general(
            jnp.concatenate([high, low], axis=0), band, dims, preferred_element_type=jnp.float32
        )
        energy = energy[: 2 * halves * n] + energy[2 * halves * n :]
        factor = scale * mask_s[chip * own + i].astype(jnp.float32)
        inv[i] = factor / jnp.sqrt(energy + 1e-06)
        return carry

    lax.fori_loop(0, own, frame, 0, unroll=own)

    for s in order:
        landed(tpair[s].at[pl.ds(0, chips // 2 - 1)], qr_sem.at[s])
        for j in range(kk):
            got = tpair[s][place(s, lax.div(plan_ref[s], 2)), j]
            got = got.astype(jnp.float32)
            tmpl[...] = jnp.concatenate([got, jnp.zeros((own, width * LANES - taps), jnp.float32)], axis=1)
            energy = jnp.sum(got * got, axis=1, keepdims=True)
            wts[...] = jnp.broadcast_to(1.0 / jnp.sqrt(energy + 1e-06), (own, part))

            def channel(i, total):
                base = jnp.broadcast_to(tmpl[pl.ds(i, 1), :], (16, width * LANES)).astype(jnp.bfloat16)
                base = jnp.concatenate([base] * (part // 16), axis=0)
                taps_of = pltpu.roll(base, 0, 1, stride=1, stride_axis=0)
                raw = lax.dot_general(frames[i], taps_of, dims, preferred_element_type=jnp.float32)
                return total + raw * inv[i] * wts[pl.ds(i, 1), :]

            total = lax.fori_loop(0, own, channel, jnp.zeros((2 * halves * n, part), jnp.float32), unroll=own)
            total = jnp.concatenate([total[: halves * n], total[halves * n :]], axis=1)
            at = (s * kk + j) * halves * n
            acc[at : at + halves * n, :] = total

    for d in range(n):
        osend[d] = acc[pl.ds(d, rows, stride=n), :]
    orecv[me] = osend[me]

    def give(d):
        return push(osend.at[d], orecv.at[me], os_sem, or_sem, d)

    @pl.loop(0, me)
    def _(d):
        give(d).start()

    @pl.loop(me + 1, n)
    def _(d):
        give(d).start()

    landed(orecv.at[pl.ds(0, n - 1)], or_sem)

    totals = jnp.sum(orecv[...].reshape(chips, 2, rows, LANES), axis=0)
    for c in range(2):
        for s in range(steps):
            for j in range(kk):
                for h in range(halves):
                    r = (s * kk + j) * halves + h
                    out_ref[s, c * kk + j, h * LANES : (h + 1) * LANES] = totals[c, r]

    for s in range(steps):
        across(s).wait_send()
        to_twin(s).wait_send()
        sent(pair_out.at[s, pl.ds(0, chips // 2 - 1)], qs_sem.at[s])
    sent(rrecv.at[0, others], rs_sem)
    forward.wait_send()
    sent(osend.at[pl.ds(0, n - 1)], os_sem)


def shards(records, bank, plan, template_ids, channel_mask):
    n = lax.axis_size("tm")
    chips = n // 2
    steps, kcount = template_ids.shape
    chans, block = records.shape
    slots, _, taps = bank.shape
    kk = kcount // 2
    own = up(-(-chans // chips), 8)
    if own * chips != chans:
        more = own * chips - chans
        records = jnp.pad(records, ((0, more), (0, 0)))
        bank = jnp.pad(bank, ((0, 0), (0, more), (0, 0)))
        channel_mask = jnp.pad(channel_mask, (0, more))
    halves = block // LANES
    part = LANES // 2
    width = up(part + taps - 1, LANES) // LANES
    vmem = pl.BlockSpec(memory_space=pltpu.VMEM)
    hbm = pl.BlockSpec(memory_space=pl.ANY)
    f32, bf16 = jnp.float32, jnp.bfloat16
    dma = pltpu.SemaphoreType.DMA
    extra = -(-(halves + width - 1) // halves)
    rows = steps * kk * halves
    piece = (kk, own, taps)
    return pl.pallas_call(
        functools.partial(kernel, n, steps, kk, taps),
        out_shape=jax.ShapeDtypeStruct((steps, kcount, block), f32),
        in_specs=[hbm] * 6,
        out_specs=vmem,
        scratch_shapes=[
            pltpu.SMEM((steps,), jnp.int32),
            pltpu.SMEM((kcount, steps), jnp.int32),
            pltpu.SMEM(channel_mask.shape, jnp.int32),
            pltpu.VMEM((1, channel_mask.shape[0]), jnp.int32),
            pltpu.VMEM(bank.shape, bf16),
            pltpu.VMEM((steps, 2, chips // 2, *piece), bf16),
            pltpu.VMEM((steps, 2, chips // 2, *piece), bf16),
            pltpu.VMEM((steps, 2, chips // 2, *piece), bf16),
            pltpu.VMEM((steps, chips // 2, *piece), bf16),
            pltpu.VMEM((steps, chips // 2, *piece), bf16),
            [pltpu.VMEM((chips // 2, *piece), bf16)] * steps,
            pltpu.VMEM((2, chips, own, block), bf16),
            pltpu.VMEM((halves, (n + extra) * own, LANES), f32),
            pltpu.VMEM((own, 2 * halves * n, width * LANES), bf16),
            pltpu.VMEM((own, 2 * halves * n, part), f32),
            pltpu.VMEM((own, width * LANES), f32),
            pltpu.VMEM((own, part), f32),
            pltpu.VMEM((rows * n, LANES), f32),
            pltpu.VMEM((n, rows, LANES), f32),
            pltpu.VMEM((2 * chips, rows, LANES), f32),
            pltpu.SemaphoreType.REGULAR((chips,)),
            dma((4,)), dma(()), dma(()), dma(()), dma(()), dma(()), dma((steps,)), dma((steps,)), dma((steps,)),
            dma((steps,)), dma((steps,)), dma((steps,)), dma(()), dma(()),
        ],
        compiler_params=pltpu.CompilerParams(
            collective_id=0, has_side_effects=True, vmem_limit_bytes=60 * 1024 * 1024
        ),
        name="detect",
    )(plan, template_ids.T, channel_mask, channel_mask.reshape(1, -1), records, bank)


def solution(mesh):
    placed = (
        P("groups", "tm"),
        P("tm", "groups", None),
        P("groups"),
        P("groups", None),
        P("groups"),
    )
    return jax.shard_map(
        shards, mesh=mesh, in_specs=placed, out_specs=P("groups", None, "tm"), check_vma=False
    )
```

time: 23.9 us -> 22 us (0.921)
  Pallas kernels: 22.3 us -> 20.5 us
    pallas_call x1, Pallas kernels: 22.3 us -> 20.5 us  [shards(): pl.pallas_call(functools.partial(kernel, n, steps, kk, taps), out_shape=j...]
where the time goes in v3:
time: 22 us; the launch traced here: 21.8 us
  Pallas kernels  20.5 us (93%)
  local copies, waits for them, and re-layouts  1.29 us (6%)
    pallas_call x1, Pallas kernels, shards(): pl.pallas_call(functools.partial(kernel, n, steps, kk, taps), out_shape=j...  20.5 us
    unnamed x1, local copies, waits for them, and re-layouts  1.29 us

profile of v3, /device:TPU:0, one launch (start us, length us, event | category | flops | bytes accessed | tf_op | source)
XLA Modules:
  0.0 21.8 jit_solution(3985739132390826666)
XLA Ops:
  0.0 20.5 %detect.1 = f32[3,2,256]{2,1,0:T(2,128)} custom-call(s32[3]{0:T(128)} %plan_in.1, s32[2,3]{1,0:T(2,128)} %bitcast.3, s32[192]{0:T(256)} %mask_in.1, s32[1,192]{1,0:T(1,128)} %bitcast.2, bf16[192,256]{1,0:T(8,128)(2,1)} %rec_ref.1, bf16[16,192,240]{2,1,0:T(8,128)(2,1)} %bank_ref.1), custom_call_target="tpu_custom_call" | custom-call | tf_op jit(solution)/shard_map/detect/pallas_call | solution.py:289
  20.5 1.3 %copy.7 = f32[3,2,256]{2,1,0:T(2,128)} copy(f32[3,2,256]{2,1,0:T(2,128)} %detect.1) | data formatting | bytes 12288

commit v4 on v3

--- a/solution.py
+++ b/solution.py
@@ -21,7 +21,7 @@
     n, steps, kk, taps,
     plan_in, ids_in, mask_in, row_in, rec_ref, bank_ref, out_ref,
     plan_ref, ids_ref, mask_s, mask_v, bank_v, tsend, tpart, tcomb, pair_in, pair_out, tpair, rrecv,
-    xs, frames, inv, tmpl, wts, acc, osend, orecv,
+    xs, frames, inv, tmpl, wts, acc, osend,
     ready, few_sem, bank_sem, rs_sem, rr_sem, fs_sem, fr_sem, cs_sem, cr_sem, ps_sem, pr_sem,
     qs_sem, qr_sem, os_sem, or_sem,
 ):
@@ -161,7 +161,7 @@
                 spread(s, i).start()
 
     keep.wait()
-    rows = steps * kk * halves
+    rows = steps * kk
     others = pl.ds(0, chips - 1)
 
     for s in range(steps):
@@ -230,11 +230,11 @@
             acc[at : at + halves * n, :] = total
 
     for d in range(n):
-        osend[d] = acc[pl.ds(d, rows, stride=n), :]
-    orecv[me] = osend[me]
+        for h in range(halves):
+            osend[d, :, h * LANES : (h + 1) * LANES] = acc[pl.ds(h * n + d, rows, stride=halves * n), :]
 
     def give(d):
-        return push(osend.at[d], orecv.at[me], os_sem, or_sem, d)
+        return push(osend.at[d], out_ref.at[core * chips + chip], os_sem, or_sem, d)
 
     @pl.loop(0, me)
     def _(d):
@@ -244,16 +244,8 @@
     def _(d):
         give(d).start()
 
-    landed(orecv.at[pl.ds(0, n - 1)], or_sem)
-
-    totals = jnp.sum(orecv[...].reshape(chips, 2, rows, LANES), axis=0)
-    for c in range(2):
-        for s in range(steps):
-            for j in range(kk):
-                for h in range(halves):
-                    r = (s * kk + j) * halves + h
-                    out_ref[s, c * kk + j, h * LANES : (h + 1) * LANES] = totals[c, r]
-
+    mine = pltpu.make_async_copy(osend.at[me], out_ref.at[core * chips + chip], bank_sem)
+    mine.start()
     for s in range(steps):
         across(s).wait_send()
         to_twin(s).wait_send()
@@ -261,6 +253,8 @@
     sent(rrecv.at[0, others], rs_sem)
     forward.wait_send()
     sent(osend.at[pl.ds(0, n - 1)], os_sem)
+    mine.wait()
+    landed(out_ref.at[pl.ds(0, n - 1)], or_sem)
 
 
 def shards(records, bank, plan, template_ids, channel_mask):
@@ -279,18 +273,17 @@
     halves = block // LANES
     part = LANES // 2
     width = up(part + taps - 1, LANES) // LANES
-    vmem = pl.BlockSpec(memory_space=pltpu.VMEM)
     hbm = pl.BlockSpec(memory_space=pl.ANY)
     f32, bf16 = jnp.float32, jnp.bfloat16
     dma = pltpu.SemaphoreType.DMA
     extra = -(-(halves + width - 1) // halves)
-    rows = steps * kk * halves
+    rows = steps * kk
     piece = (kk, own, taps)
-    return pl.pallas_call(
+    parts = pl.pallas_call(
         functools.partial(kernel, n, steps, kk, taps),
-        out_shape=jax.ShapeDtypeStruct((steps, kcount, block), f32),
+        out_shape=jax.ShapeDtypeStruct((n, rows, block), f32),
         in_specs=[hbm] * 6,
-        out_specs=vmem,
+        out_specs=hbm,
         scratch_shapes=[
             pltpu.SMEM((steps,), jnp.int32),
             pltpu.SMEM((kcount, steps), jnp.int32),
@@ -309,9 +302,8 @@
             pltpu.VMEM((own, 2 * halves * n, part), f32),
             pltpu.VMEM((own, width * LANES), f32),
             pltpu.VMEM((own, part), f32),
-            pltpu.VMEM((rows * n, LANES), f32),
-            pltpu.VMEM((n, rows, LANES), f32),
-            pltpu.VMEM((2 * chips, rows, LANES), f32),
+            pltpu.VMEM((rows * halves * n, LANES), f32),
+            pltpu.VMEM((n, rows, block), f32),
             pltpu.SemaphoreType.REGULAR((chips,)),
             dma((4,)), dma(()), dma(()), dma(()), dma(()), dma(()), dma((steps,)), dma((steps,)), dma((steps,)),
             dma((steps,)), dma((steps,)), dma((steps,)), dma(()), dma(()),
@@ -321,6 +313,8 @@
         ),
         name="detect",
     )(plan, template_ids.T, channel_mask, channel_mask.reshape(1, -1), records, bank)
+    sums = jnp.sum(parts.reshape(2, chips, steps, kk, block), axis=1)
+    return jnp.swapaxes(sums, 0, 1).reshape(steps, kcount, block)
 
 
 def solution(mesh):

time: 22 us -> 21.6 us (0.982)
  other arithmetic: 0 us -> 0.86 us
  local copies, waits for them, and re-layouts: 1.29 us -> 0.6 us
  Pallas kernels: 20.5 us -> 20 us
    unnamed x1 -> x0, local copies, waits for them, and re-layouts: 1.29 us -> none
    reduce_sum x0 -> x1, other arithmetic: none -> 0.86 us  [shards(): sums = jnp.sum(parts.reshape(2, chips, steps, kk, block), axis=1)]
    reshape x0 -> x1, local copies, waits for them, and re-layouts: none -> 0.6 us  [shards(): return jnp.swapaxes(sums, 0, 1).reshape(steps, kcount, block)]
    pallas_call x1, Pallas kernels: 20.5 us -> 20 us  [shards(): pl.pallas_call(functools.partial(kernel, n, steps, kk, taps), out_shape=j...]
where the time goes in v4:
time: 21.6 us; the launch traced here: 21.5 us
  Pallas kernels  20 us (93%)
  other arithmetic  0.86 us (4%)
  local copies, waits for them, and re-layouts  0.6 us (3%)
    pallas_call x1, Pallas kernels, shards(): pl.pallas_call(functools.partial(kernel, n, steps, kk, taps), out_shape=j...  20 us
    reduce_sum x1, other arithmetic, shards(): sums = jnp.sum(parts.reshape(2, chips, steps, kk, block), axis=1)  0.86 us
    reshape x1, local copies, waits for them, and re-layouts, shards(): return jnp.swapaxes(sums, 0, 1).reshape(steps, kcount, block)  0.6 us

profile of v4, /device:TPU:0, one launch (start us, length us, event | category | flops | bytes accessed | tf_op | source)
XLA Modules:
  0.0 21.5 jit_solution(1271381843360111076)
XLA Ops:
  0.0 20.0 %detect.1 = f32[16,3,256]{2,1,0:T(4,128)} custom-call(s32[3]{0:T(128)} %plan_in.1, s32[2,3]{1,0:T(2,128)} %bitcast.11, s32[192]{0:T(256)} %mask_in.1, s32[1,192]{1,0:T(1,128)} %bitcast.10, bf16[192,256]{1,0:T(8,128)(2,1)} %rec_ref.1, bf16[16,192,240]{2,1,0:T(8,128)(2,1)} %bank_ref.1), custom_call_target="tpu_custom_call" | custom-call | tf_op jit(solution)/shard_map/detect/pallas_call | solution.py:282
  20.0 0.9 %bitcast_reduce_fusion = f32[2,3,256]{2,1,0:T(4,128)S(1)} fusion(f32[16,3,256]{2,1,0:T(4,128)} %detect.1), kind=kLoop, calls=%fused_computation | loop fusion | flops 10752 | bytes 55296 | tf_op jit(solution)/shard_map/reduce_sum | solution.py:316
  20.9 0.6 %copy.6 = f32[3,2,256]{2,1,0:T(2,128)} copy(f32[3,2,256]{2,0,1:T(4,128)S(1)} %bitcast.9) | data formatting | bytes 12288 | tf_op jit(solution)/shard_map/reshape | solution.py:317

commit v5 on v4

--- a/solution.py
+++ b/solution.py
@@ -89,15 +89,19 @@
         return push(rows_of(q), rrecv.at[core, chip], rs_sem, rr_sem, 2 * q + core)
 
     def across(s):
-        return push(tsend.at[s], tpart.at[s], cs_sem.at[s], cr_sem.at[s], partner)
+        return push(tsend.at[s], tpart.at[s], cs_sem, cr_sem.at[s], partner)
 
     def to_twin(s):
-        return push(tcomb.at[s, 1 - side(s, chip)], pair_in.at[s], ps_sem.at[s], pr_sem.at[s], 2 * twin(s) + core)
+        return push(tcomb.at[s, 1 - side(s, chip)], pair_in.at[s], ps_sem, pr_sem.at[s], 2 * twin(s) + core)
 
     def spread(s, i):
         return push(
-            pair_out.at[s, i], tpair[s].at[place(s, chip)], qs_sem.at[s], qr_sem.at[s], 2 * chip_at(s, i) + core
+            pair_out.at[s, i], tpair[s].at[place(s, chip)], qs_sem, qr_sem.at[s], 2 * chip_at(s, i) + core
         )
+
+    @pl.loop(0, chip)
+    def _(q):
+        tell(ready.at[chip], 2 * q + core)
 
     for copy in few:
         copy.wait()
@@ -111,10 +115,6 @@
 
     @pl.loop(0, chip)
     def _(q):
-        tell(ready.at[chip], 2 * q + core)
-
-    @pl.loop(0, chip)
-    def _(q):
         send_records(q).start()
 
     for s in order:
@@ -148,7 +148,13 @@
 
         send_records(q).start()
 
+    others = pl.ds(0, chips - 1)
+    forward = push(rrecv.at[core], rrecv.at[core], fs_sem, fr_sem, partner)
     for s in order:
+        if s == order[-1]:
+            keep.wait()
+            landed(rrecv.at[0, others], rr_sem)
+            forward.start()
         landed(pair_in.at[s], pr_sem.at[s])
         theirs = lax.div(plan_ref[s], 2) == twin(s)
         for i in range(chips // 2):
@@ -160,15 +166,10 @@
             def _():
                 spread(s, i).start()
 
-    keep.wait()
     rows = steps * kk
-    others = pl.ds(0, chips - 1)
 
     for s in range(steps):
         tpair[s][place(s, chip)] = pair_out[s, place(s, chip)]
-    landed(rrecv.at[0, others], rr_sem)
-    forward = push(rrecv.at[core], rrecv.at[core], fs_sem, fr_sem, partner)
-    forward.start()
     forward.wait_recv()
 
     for v in range(halves):
@@ -246,10 +247,9 @@
 
     mine = pltpu.make_async_copy(osend.at[me], out_ref.at[core * chips + chip], bank_sem)
     mine.start()
-    for s in range(steps):
-        across(s).wait_send()
-        to_twin(s).wait_send()
-        sent(pair_out.at[s, pl.ds(0, chips // 2 - 1)], qs_sem.at[s])
+    sent(tsend, cs_sem)
+    sent(pair_in, ps_sem)
+    sent(pair_out.at[:, pl.ds(0, chips // 2 - 1)], qs_sem)
     sent(rrecv.at[0, others], rs_sem)
     forward.wait_send()
     sent(osend.at[pl.ds(0, n - 1)], os_sem)
@@ -305,8 +305,8 @@
             pltpu.VMEM((rows * halves * n, LANES), f32),
             pltpu.VMEM((n, rows, block), f32),
             pltpu.SemaphoreType.REGULAR((chips,)),
-            dma((4,)), dma(()), dma(()), dma(()), dma(()), dma(()), dma((steps,)), dma((steps,)), dma((steps,)),
-            dma((steps,)), dma((steps,)), dma((steps,)), dma(()), dma(()),
+            dma((4,)), dma(()), dma(()), dma(()), dma(()), dma(()), dma(()), dma((steps,)), dma(()),
+            dma((steps,)), dma(()), dma((steps,)), dma(()), dma(()),
         ],
         compiler_params=pltpu.CompilerParams(
             collective_id=0, has_side_effects=True, vmem_limit_bytes=60 * 1024 * 1024

time: 21.6 us -> 21.4 us (level)
  Pallas kernels: 20 us -> 19.7 us
    pallas_call x1, Pallas kernels: 20 us -> 19.7 us  [shards(): pl.pallas_call(functools.partial(kernel, n, steps, kk, taps), out_shape=j...]
where the time goes in v5:
time: 21.4 us; the launch traced here: 21.2 us
  Pallas kernels  19.7 us (92%)
  other arithmetic  0.86 us (4%)
  local copies, waits for them, and re-layouts  0.6 us (3%)
    pallas_call x1, Pallas kernels, shards(): pl.pallas_call(functools.partial(kernel, n, steps, kk, taps), out_shape=j...  19.7 us
    reduce_sum x1, other arithmetic, shards(): sums = jnp.sum(parts.reshape(2, chips, steps, kk, block), axis=1)  0.86 us
    reshape x1, local copies, waits for them, and re-layouts, shards(): return jnp.swapaxes(sums, 0, 1).reshape(steps, kcount, block)  0.6 us

profile of v5, /device:TPU:0, one launch (start us, length us, event | category | flops | bytes accessed | tf_op | source)
XLA Modules:
  0.0 21.2 jit_solution(4039938449756803436)
XLA Ops:
  0.0 19.7 %detect.1 = f32[16,3,256]{2,1,0:T(4,128)} custom-call(s32[3]{0:T(128)} %plan_in.1, s32[2,3]{1,0:T(2,128)} %bitcast.11, s32[192]{0:T(256)} %mask_in.1, s32[1,192]{1,0:T(1,128)} %bitcast.10, bf16[192,256]{1,0:T(8,128)(2,1)} %rec_ref.1, bf16[16,192,240]{2,1,0:T(8,128)(2,1)} %bank_ref.1), custom_call_target="tpu_custom_call" | custom-call | tf_op jit(solution)/shard_map/detect/pallas_call | solution.py:282
  19.7 0.9 %bitcast_reduce_fusion = f32[2,3,256]{2,1,0:T(4,128)S(1)} fusion(f32[16,3,256]{2,1,0:T(4,128)} %detect.1), kind=kLoop, calls=%fused_computation | loop fusion | flops 10752 | bytes 55296 | tf_op jit(solution)/shard_map/reduce_sum | solution.py:316
  20.6 0.6 %copy.6 = f32[3,2,256]{2,1,0:T(2,128)} copy(f32[3,2,256]{2,0,1:T(4,128)S(1)} %bitcast.9) | data formatting | bytes 12288 | tf_op jit(solution)/shard_map/reshape | solution.py:317

commit v6 on v5

--- a/solution.py
+++ b/solution.py
@@ -209,23 +209,31 @@
 
     lax.fori_loop(0, own, frame, 0, unroll=own)
 
-    for s in order:
-        landed(tpair[s].at[pl.ds(0, chips // 2 - 1)], qr_sem.at[s])
-        for j in range(kk):
-            got = tpair[s][place(s, lax.div(plan_ref[s], 2)), j]
-            got = got.astype(jnp.float32)
-            tmpl[...] = jnp.concatenate([got, jnp.zeros((own, width * LANES - taps), jnp.float32)], axis=1)
+    for group in [[s] for s in order]:
+        turns = [(s, j) for s in group for j in range(kk)]
+        for s, j in turns:
+            if j == 0:
+                landed(tpair[s].at[pl.ds(0, chips // 2 - 1)], qr_sem.at[s])
+            r = s * kk + j
+            got = tpair[s][place(s, lax.div(plan_ref[s], 2)), j].astype(jnp.float32)
+            tmpl[r] = jnp.concatenate([got, jnp.zeros((own, width * LANES - taps), jnp.float32)], axis=1)
             energy = jnp.sum(got * got, axis=1, keepdims=True)
-            wts[...] = jnp.broadcast_to(1.0 / jnp.sqrt(energy + 1e-06), (own, part))
-
-            def channel(i, total):
-                base = jnp.broadcast_to(tmpl[pl.ds(i, 1), :], (16, width * LANES)).astype(jnp.bfloat16)
+            wts[r] = jnp.broadcast_to(1.0 / jnp.sqrt(energy + 1e-06), (own, part))
+
+        def channel(i, totals):
+            sums = []
+            for (s, j), total in zip(turns, totals):
+                r = s * kk + j
+                base = jnp.broadcast_to(tmpl[r, pl.ds(i, 1), :], (16, width * LANES)).astype(jnp.bfloat16)
                 base = jnp.concatenate([base] * (part // 16), axis=0)
                 taps_of = pltpu.roll(base, 0, 1, stride=1, stride_axis=0)
                 raw = lax.dot_general(frames[i], taps_of, dims, preferred_element_type=jnp.float32)
-                return total + raw * inv[i] * wts[pl.ds(i, 1), :]
-
-            total = lax.fori_loop(0, own, channel, jnp.zeros((2 * halves * n, part), jnp.float32), unroll=own)
+                sums.append(total + raw * inv[i] * wts[r, pl.ds(i, 1), :])
+            return tuple(sums)
+
+        none = jnp.zeros((2 * halves * n, part), jnp.float32)
+        totals = lax.fori_loop(0, own, channel, (none,) * len(turns), unroll=own)
+        for (s, j), total in zip(turns, totals):
             total = jnp.concatenate([total[: halves * n], total[halves * n :]], axis=1)
             at = (s * kk + j) * halves * n
             acc[at : at + halves * n, :] = total
@@ -300,8 +308,8 @@
             pltpu.VMEM((halves, (n + extra) * own, LANES), f32),
             pltpu.VMEM((own, 2 * halves * n, width * LANES), bf16),
             pltpu.VMEM((own, 2 * halves * n, part), f32),
-            pltpu.VMEM((own, width * LANES), f32),
-            pltpu.VMEM((own, part), f32),
+            pltpu.VMEM((steps * kk, own, width * LANES), f32),
+            pltpu.VMEM((steps * kk, own, part), f32),
             pltpu.VMEM((rows * halves * n, LANES), f32),
             pltpu.VMEM((n, rows, block), f32),
             pltpu.SemaphoreType.REGULAR((chips,)),

time: 21.4 us -> 21.4 us (level)
  no operation moved by 1% of the time
where the time goes in v6:
time: 21.4 us; the launch traced here: 21.2 us
  Pallas kernels  19.7 us (92%)
  other arithmetic  0.86 us (4%)
  local copies, waits for them, and re-layouts  0.6 us (3%)
    pallas_call x1, Pallas kernels, shards(): pl.pallas_call(functools.partial(kernel, n, steps, kk, taps), out_shape=j...  19.7 us
    reduce_sum x1, other arithmetic, shards(): sums = jnp.sum(parts.reshape(2, chips, steps, kk, block), axis=1)  0.86 us
    reshape x1, local copies, waits for them, and re-layouts, shards(): return jnp.swapaxes(sums, 0, 1).reshape(steps, kcount, block)  0.6 us

profile of v6, /device:TPU:0, one launch (start us, length us, event | category | flops | bytes accessed | tf_op | source)
XLA Modules:
  0.0 21.2 jit_solution(16778260078099361350)
XLA Ops:
  0.0 19.7 %detect.1 = f32[16,3,256]{2,1,0:T(4,128)} custom-call(s32[3]{0:T(128)} %plan_in.1, s32[2,3]{1,0:T(2,128)} %bitcast.11, s32[192]{0:T(256)} %mask_in.1, s32[1,192]{1,0:T(1,128)} %bitcast.10, bf16[192,256]{1,0:T(8,128)(2,1)} %rec_ref.1, bf16[16,192,240]{2,1,0:T(8,128)(2,1)} %bank_ref.1), custom_call_target="tpu_custom_call" | custom-call | tf_op jit(solution)/shard_map/detect/pallas_call | solution.py:290
  19.7 0.9 %bitcast_reduce_fusion = f32[2,3,256]{2,1,0:T(4,128)S(1)} fusion(f32[16,3,256]{2,1,0:T(4,128)} %detect.1), kind=kLoop, calls=%fused_computation | loop fusion | flops 10752 | bytes 55296 | tf_op jit(solution)/shard_map/reduce_sum | solution.py:324
  20.6 0.6 %copy.6 = f32[3,2,256]{2,1,0:T(2,128)} copy(f32[3,2,256]{2,0,1:T(4,128)S(1)} %bitcast.9) | data formatting | bytes 12288 | tf_op jit(solution)/shard_map/reshape | solution.py:325

commit v7 on v6

--- a/solution.py
+++ b/solution.py
@@ -66,6 +66,13 @@
     def landed(ref, sem):
         push(ref, ref, sem, sem, partner).wait_recv()
 
+    barrier = pltpu.get_barrier_semaphore()
+    tell(barrier, partner)
+
+    @pl.loop(chip + 1, chips)
+    def _(q):
+        tell(barrier, 2 * q + core)
+
     fetch = pltpu.make_async_copy(bank_ref, bank_v, bank_sem)
     fetch.start()
     few = [
@@ -74,13 +81,6 @@
     ]
     for copy in few:
         copy.start()
-    barrier = pltpu.get_barrier_semaphore()
-    tell(barrier, partner)
-
-    @pl.loop(chip + 1, chips)
-    def _(q):
-        tell(barrier, 2 * q + core)
-
     pl.semaphore_wait(barrier, 1 + chip)
     def rows_of(q):
         return rec_ref.at[pl.ds(pl.multiple_of(q * own, 8), own)]

time: 21.4 us -> 21.4 us (level)
  no operation moved by 1% of the time
where the time goes in v7:
time: 21.4 us; the launch traced here: 21.2 us
  Pallas kernels  19.7 us (92%)
  other arithmetic  0.86 us (4%)
  local copies, waits for them, and re-layouts  0.6 us (3%)
    pallas_call x1, Pallas kernels, shards(): pl.pallas_call(functools.partial(kernel, n, steps, kk, taps), out_shape=j...  19.7 us
    reduce_sum x1, other arithmetic, shards(): sums = jnp.sum(parts.reshape(2, chips, steps, kk, block), axis=1)  0.86 us
    reshape x1, local copies, waits for them, and re-layouts, shards(): return jnp.swapaxes(sums, 0, 1).reshape(steps, kcount, block)  0.6 us

profile of v7, /device:TPU:0, one launch (start us, length us, event | category | flops | bytes accessed | tf_op | source)
XLA Modules:
  0.0 21.2 jit_solution(7922148628394719685)
XLA Ops:
  0.0 19.7 %detect.1 = f32[16,3,256]{2,1,0:T(4,128)} custom-call(s32[3]{0:T(128)} %plan_in.1, s32[2,3]{1,0:T(2,128)} %bitcast.11, s32[192]{0:T(256)} %mask_in.1, s32[1,192]{1,0:T(1,128)} %bitcast.10, bf16[192,256]{1,0:T(8,128)(2,1)} %rec_ref.1, bf16[16,192,240]{2,1,0:T(8,128)(2,1)} %bank_ref.1), custom_call_target="tpu_custom_call" | custom-call | tf_op jit(solution)/shard_map/detect/pallas_call | solution.py:290
  19.7 0.9 %bitcast_reduce_fusion = f32[2,3,256]{2,1,0:T(4,128)S(1)} fusion(f32[16,3,256]{2,1,0:T(4,128)} %detect.1), kind=kLoop, calls=%fused_computation | loop fusion | flops 10752 | bytes 55296 | tf_op jit(solution)/shard_map/reduce_sum | solution.py:324
  20.6 0.6 %copy.6 = f32[3,2,256]{2,1,0:T(2,128)} copy(f32[3,2,256]{2,0,1:T(4,128)S(1)} %bitcast.9) | data formatting | bytes 12288 | tf_op jit(solution)/shard_map/reshape | solution.py:325
